TPU v7x, 256 devices: a whole 4x4x8 slice. The times are simulated.
256 devices in a mesh: dp: 2 (over x_lo), context: 8 (over z), tensor: 16 (over y, x_hi, core).
Axes of the slice: x: 4 (x_hi: 2, x_lo: 2; x = x_hi * 2 + x_lo), y: 4, z: 8, core: 2. Of those that a mesh axis runs over, the one named last changes fastest.
Arguments:
- activations: bfloat16 [2, 4096, 4096], P('dp', ('context', 'tensor')), may hold values from -60 to 60
- in_weight: bfloat16 [4096, 3, 4096], P('dp', None, 'tensor'), may hold values from -0.09375 to 0.09375
- out_weight: bfloat16 [4096, 4096], P('tensor', 'dp'), may hold values from -0.09375 to 0.09375
- short_filter: float32 [3, 3, 4096], P(None, None, 'tensor'), may hold values from -2 to 2
- mixer_filter: float32 [128, 256], P(None, 'tensor'), may hold values from -0.5 to 0.5
- cotangent: bfloat16 [2, 4096, 4096], P('dp', ('context', 'tensor')), may hold values from -6 to 6
Outputs:
- block_out: bfloat16 [2, 4096, 4096], P('dp', ('context', 'tensor'))
- grad_input: bfloat16 [2, 4096, 4096], P('dp', ('context', 'tensor'))
- grad_in_weight: bfloat16 [4096, 3, 4096], P(('dp', 'context'), None, 'tensor')
- grad_out_weight: bfloat16 [4096, 4096], P('tensor', ('dp', 'context'))
- grad_short: float32 [3, 3, 4096], P(None, None, 'tensor')
- grad_mixer: float32 [128, 256], P(None, 'tensor')
All inputs are finite; a program needn't handle non-finite values.
Results may differ from a plain program's by a relative error of at most 0.019.
Values may be sent and summed in bfloat16 or wider, within the bound.
A program may use at most 128 MiB of HBM per device.

v0:
```python
import jax
import jax.numpy as jnp
from jax import lax
from jax.sharding import PartitionSpec as P

EPS = 1e-05


def from_behind(value, axis, steps):
    count = lax.axis_size(axis)
    initial, last = (max(0, -steps), min(count, count - steps))
    return lax.ppermute(value, axis, [(source, source + steps) for source in range(initial, last)])


def pair_gather(value, axis, dim):
    count = lax.axis_size(axis)
    index = lax.axis_index(axis)
    parts = [value]
    for step in range(1, count):
        parts.append(lax.ppermute(value, axis, [(i, (i + step) % count) for i in range(count)]))
    shape = list(value.shape)
    size = shape[dim]
    shape[dim] = size * count
    full = jnp.zeros(shape, value.dtype)
    for step, part in enumerate(parts):
        start = [0] * len(shape)
        start[dim] = (index - step) % count * size
        full = lax.dynamic_update_slice(full, part, start)
    return full


def scatter_sum(value, axis, dim):
    count = lax.axis_size(axis)
    shape = value.shape
    split = shape[:dim] + (count, shape[dim] // count) + shape[dim + 1 :]
    pieces = lax.all_to_all(value.reshape(split), axis, dim, 0)
    return jnp.sum(pieces.astype(jnp.float32), axis=0)


def skew_table(base, span):
    groups = base.shape[0]
    padded = jnp.concatenate([base, jnp.zeros((groups, span + 1), jnp.float32)], axis=1)
    tiled = jnp.tile(padded[:, None, :], (1, span, 1)).reshape(groups, span * (2 * span + 1))
    return tiled[:, : span * 2 * span].reshape(groups, span, 2 * span)


def band_windows(extended, span, groups):
    chans = extended.shape[1]
    padded = jnp.concatenate([extended, jnp.zeros((1, chans), jnp.float32)], 0)
    blocks = padded.shape[0] // span
    padded = padded.reshape(blocks, span, groups, chans // groups)
    return jnp.concatenate([padded[:-1], padded[1:]], axis=1)


def band_apply(table, extended, span):
    groups = table.shape[0]
    chans = extended.shape[1]
    windows = band_windows(extended, span, groups)
    result = jnp.einsum("gtu,bugc->btgc", table, windows, precision=lax.Precision.HIGHEST)
    return result.reshape(windows.shape[0] * span, chans)


def band_grad(left, extended, span, groups):
    rows, chans = left.shape
    lhs = left.reshape(rows // span, span, groups, chans // groups)
    windows = band_windows(extended, span, groups)
    prods = jnp.einsum("btgc,bugc->gtu", lhs, windows, precision=lax.Precision.HIGHEST)
    flat = jnp.concatenate(
        [prods.reshape(groups, span * 2 * span), jnp.zeros((groups, span), jnp.float32)], axis=1
    )
    skewed = flat.reshape(groups, span, 2 * span + 1).sum(axis=1)
    return jnp.flip(skewed[:, :span], axis=1).T


def short_apply(filters, extended, rows):
    taps = filters.shape[1]
    total = jnp.zeros((rows,) + extended.shape[1:], jnp.float32)
    for tap in range(taps):
        total = total + filters[:, tap][None] * extended[taps - 1 - tap : taps - 1 - tap + rows]
    return total


def per_device(activations, in_weight, out_weight, short_filter, mixer_filter, cotangent):
    rows_own = activations.shape[1]
    width = activations.shape[2]
    rows = rows_own * lax.axis_size("tensor")
    span = mixer_filter.shape[0]
    groups = mixer_filter.shape[1]
    taps = short_filter.shape[1]
    chans = short_filter.shape[2]
    own = activations[0].astype(jnp.float32)
    inverse = lax.rsqrt(jnp.mean(own * own, axis=-1, keepdims=True) + EPS)
    normed = (own * inverse).astype(jnp.bfloat16)
    slab = lax.all_gather(normed, "tensor", axis=0, tiled=True)
    full_in = pair_gather(in_weight, "dp", 0)
    full_out = pair_gather(out_weight, "dp", 1)
    in_flat = full_in.reshape(width, 3 * chans)
    projected = (
        jnp.dot(slab, in_flat, preferred_element_type=jnp.float32)
        .astype(jnp.bfloat16)
        .reshape(rows, 3, chans)
    )
    proj_wide = projected.astype(jnp.float32)
    table_fwd = skew_table(jnp.flip(mixer_filter, axis=0).T, span)
    table_back = skew_table(mixer_filter.T, span)
    short_rim = from_behind(projected[rows - taps + 1 :], "context", 1)
    proj_ext = jnp.concatenate([short_rim.astype(jnp.float32), proj_wide], 0)
    streams = short_apply(short_filter, proj_ext, rows)
    gated = (streams[:, 1] * streams[:, 2]).astype(jnp.bfloat16)
    gate_rim = from_behind(gated[rows - span + 1 :], "context", 1)
    gate_ext = jnp.concatenate([gate_rim, gated], 0).astype(jnp.float32)
    mixed = band_apply(table_fwd, gate_ext, span)
    output_rows = (streams[:, 0] * mixed).astype(jnp.bfloat16)
    piece = output_rows
    branch = scatter_sum(
        jnp.dot(piece, full_out, preferred_element_type=jnp.float32).astype(jnp.bfloat16),
        "tensor",
        0,
    )
    block_out = (own + branch).astype(jnp.bfloat16)[None]
    cot_slab = lax.all_gather(cotangent[0], "tensor", axis=0, tiled=True)
    grad_rows = lax.dot_general(
        cot_slab, full_out, (((1,), (1,)), ((), ())), preferred_element_type=jnp.float32
    )
    out_term = lax.dot_general(
        output_rows, cot_slab, (((0,), (0,)), ((), ())), preferred_element_type=jnp.float32
    )
    grad_mix = (grad_rows * streams[:, 0]).astype(jnp.bfloat16)
    grad_mix_wide = grad_mix.astype(jnp.float32)
    mix_rim = from_behind(grad_mix[: span - 1], "context", -1)
    grad_gate = band_apply(
        table_back, jnp.concatenate([grad_mix_wide, mix_rim.astype(jnp.float32)], 0), span
    )
    mixer_term = band_grad(grad_mix_wide, gate_ext, span, groups)
    grad_streams = jnp.stack(
        [grad_rows * mixed, grad_gate * streams[:, 2], grad_gate * streams[:, 1]], axis=1
    )
    stream_rim = from_behind(grad_streams[: taps - 1], "context", -1)
    stream_ext = jnp.concatenate([grad_streams, stream_rim], 0)
    grad_proj = jnp.zeros((rows, 3, chans), jnp.float32)
    for tap in range(taps):
        grad_proj = grad_proj + short_filter[:, tap][None] * stream_ext[tap : tap + rows]
    grad_proj = grad_proj.astype(jnp.bfloat16)
    short_terms = [
        jnp.sum(grad_streams * proj_ext[taps - 1 - tap : taps - 1 - tap + rows], axis=0)
        for tap in range(taps)
    ]
    short_term = jnp.stack(short_terms, axis=1)
    grad_short, grad_mixer = lax.psum((short_term, mixer_term), ("dp", "context"))
    proj_flat = grad_proj.reshape(rows, 3 * chans)
    in_term = lax.dot_general(
        slab, proj_flat, (((0,), (0,)), ((), ())), preferred_element_type=jnp.float32
    ).reshape(width, 3, chans)
    grad_in, grad_out = (
        lax.psum_scatter(
            in_term.astype(jnp.bfloat16), ("dp", "context"), scatter_dimension=0, tiled=True
        ).astype(jnp.float32),
        lax.psum_scatter(
            out_term.astype(jnp.bfloat16), ("dp", "context"), scatter_dimension=1, tiled=True
        ).astype(jnp.float32),
    )
    piece = proj_flat
    grad_norm = scatter_sum(
        lax.dot_general(
            piece, in_flat, (((1,), (1,)), ((), ())), preferred_element_type=jnp.float32
        ).astype(jnp.bfloat16),
        "tensor",
        0,
    )
    grad_x = (
        cotangent[0].astype(jnp.float32)
        + inverse * grad_norm
        - own * inverse**3 * jnp.mean(grad_norm * own, axis=-1, keepdims=True)
    )
    grad_input = grad_x.astype(jnp.bfloat16)[None]
    return (
        block_out,
        grad_input,
        grad_in.astype(jnp.bfloat16),
        grad_out.astype(jnp.bfloat16),
        grad_short,
        grad_mixer,
    )


def solution(mesh):
    placed = (
        P("dp", ("context", "tensor"), None),
        P("dp", None, "tensor"),
        P("tensor", "dp"),
        P(None, None, "tensor"),
        P(None, "tensor"),
        P("dp", ("context", "tensor"), None),
    )
    return jax.shard_map(
        per_device,
        mesh=mesh,
        in_specs=placed,
        out_specs=(
            P("dp", ("context", "tensor"), None),
            P("dp", ("context", "tensor"), None),
            P(("dp", "context"), None, "tensor"),
            P("tensor", ("dp", "context")),
            P(None, None, "tensor"),
            P(None, "tensor"),
        ),
        check_vma=False,
    )
```

profile of v0, /device:TPU:6, one launch (start us, length us, event | category | flops | bytes accessed | tf_op | source)
XLA Modules:
  0.0 470.9 jit_solution(5357234230657179776)
XLA Ops:
  11.9 4.7 %copy.21 = bf16[2048,3,256]{0,2,1:T(8,128)(2,1)} copy(bf16[2048,3,256]{2,0,1:T(8,128)(2,1)} %param.7) | data formatting | bytes 6291456 | tf_op args[1]
  23.7 3.9 constant_dynamic-update-slice_fusion.3
  27.7 74.4 %collective-permute-done = bf16[2048,3,256]{0,2,1:T(8,128)(2,1)} collective-permute-done((bf16[2048,3,256]{0,2,1:T(8,128)(2,1)}, bf16[2048,3,256]{0,2,1:T(8,128)(2,1)}, u32[]{:S(2)}, u32[]{:S(2)}) %collective-permute-start) | collective-permute-done | bytes 3145760 | tf_op jit(solution)/shard_map/ppermute | solution.py:20
  102.0 4.1 constant_dynamic-update-slice_fusion.2
  106.1 7.5 %convolution_convert_fusion.3 = bf16[512,768]{1,0:T(8,128)(2,1)S(1)} fusion(bf16[512,4096]{1,0:T(8,128)(2,1)} %all-gather.4.cloned.1.call-done, bf16[4096,768]{0,1:T(8,128)(2,1)} %bitcast.1), kind=kOutput, calls=%fused_computation.29 | convolution fusion | flops 3221618688 | bytes 11272192 | tf_op jit(solution)/shard_map/dot_general | solution.py:99
  113.9 4.5 collective-permute-start.1
  118.4 7.8 %collective-permute-done.3 = bf16[256,2048]{1,0:T(8,128)(2,1)} collective-permute-done((bf16[256,2048]{1,0:T(8,128)(2,1)}, bf16[256,2048]{1,0:T(8,128)(2,1)}, u32[]{:S(2)}, u32[]{:S(2)}) %collective-permute-start.3) | collective-permute-done | bytes 1048608 | tf_op jit(solution)/shard_map/ppermute | solution.py:20
  130.0 4.2 multiply_add_fusion
  134.3 16.4 %all-gather.6.cloned.1.call-done = bf16[1,512,4096]{2,1,0:T(8,128)(2,1)} async-done(((bf16[1,32,4096]{2,1,0:T(8,128)(2,1)}), bf16[1,512,4096]{2,1,0:T(8,128)(2,1)}) %all-gather.6.cloned.1.call-update) | async-done | bytes 4194320 | tf_op jit(solution)/shard_map/all_gather | solution.py:121
  150.6 4.5 fusion.42
  158.5 3.9 tile.17
  172.9 3.9 fusion.15
  181.0 5.2 %collective-permute-start.2 = (bf16[127,256]{0,1:T(8,128)(2,1)}, bf16[127,256]{0,1:T(8,128)(2,1)}, u32[]{:S(2)}, u32[]{:S(2)}) collective-permute-start(bf16[127,256]{0,1:T(8,128)(2,1)} %slice_bitcast_fusion.1), channel_id=1, source_target_pairs={{0,16},{16,32},{32,48},{48,64},{64,80},{80,96},{96,112},{1,17},{17... | collective-permute-start | bytes 195080 | tf_op jit(solution)/shard_map/ppermute | solution.py:12
  190.1 3.9 tile.15
  207.6 4.3 fusion.12
  220.7 12.7 %collective-permute-done.5 = f32[2,3,256]{0,2,1:T(8,128)S(1)} collective-permute-done((f32[2,3,256]{0,2,1:T(8,128)S(1)}, f32[2,3,256]{0,2,1:T(8,128)S(1)}, u32[]{:S(2)}, u32[]{:S(2)}) %collective-permute-start.5) | collective-permute-done | bytes 6176 | tf_op jit(solution)/shard_map/ppermute | solution.py:12
  233.5 3.4 multiply_reduce_fusion.1
  237.8 5.4 %convolution_convert_fusion = bf16[4096,3,256]{2,0,1:T(8,128)(2,1)} fusion(bf16[512,4096]{1,0:T(8,128)(2,1)S(1)} %copy-done.25, bf16[512,3,256]{0,2,1:T(8,128)(2,1)S(1)} %get-tuple-element.20), kind=kOutput, calls=%fused_computation.3 | convolution fusion | flops 3224371200 | bytes 11272192 | tf_op jit(solution)/shard_map/dot_general | solution.py:151
  247.5 6.9 %all-to-all-start = ((bf16[16,32,4096]{2,1,0:T(8,128)(2,1)}), bf16[16,32,4096]{2,1,0:T(8,128)(2,1)}, u32[]{:S(2)}, u32[]{:S(2)}) async-start(bf16[16,32,4096]{2,1,0:T(8,128)(2,1)} %bitcast.143), calls=%async_computation | async-start | bytes 8388608 | tf_op jit(solution)/shard_map/all_to_all | solution.py:36
  254.4 7.8 %bitcast_convert_fusion = bf16[512,4096]{1,0:T(8,128)(2,1)} fusion(bf16[512,3,256]{0,2,1:T(8,128)(2,1)S(1)} %copy-done.18, bf16[4096,3,256]{0,2,1:T(8,128)(2,1)} %constant_dynamic-update-slice_fusion.2), kind=kOutput, calls=%fused_computation | convolution fusion | flops 3223322624 | bytes 11272192 | tf_op jit(solution)/shard_map/dot_general | solution.py:164
  262.2 113.2 %all-to-all-done = bf16[16,32,4096]{2,1,0:T(8,128)(2,1)} async-done(((bf16[16,32,4096]{2,1,0:T(8,128)(2,1)}), bf16[16,32,4096]{2,1,0:T(8,128)(2,1)}, u32[]{:S(2)}, u32[]{:S(2)}) %all-to-all-start) | async-done | bytes 4194336 | tf_op jit(solution)/shard_map/all_to_all | solution.py:36
  375.3 8.2 %all-to-all-start.1 = ((bf16[16,32,4096]{2,1,0:T(8,128)(2,1)}), bf16[16,32,4096]{2,1,0:T(8,128)(2,1)}, u32[]{:S(2)}, u32[]{:S(2)}) async-start(bf16[16,32,4096]{2,1,0:T(8,128)(2,1)} %bitcast.153), calls=%async_computation.1 | async-start | bytes 8388608 | tf_op jit(solution)/shard_map/all_to_all | solution.py:36
  387.4 3.7 reshape.148
  393.6 62.8 %all-reduce.4 = (f32[3,3,256]{2,0,1:T(4,128)S(1)}, f32[128,16]{0,1:T(8,128)}) all-reduce(f32[3,3,256]{2,0,1:T(4,128)S(1)} %pad_maximum_fusion.4, f32[128,16]{0,1:T(8,128)S(1)} %bitcast.159), channel_id=1, replica_groups=mesh['dp'=2,'context'=8,'tensor'=16] {'dp','context'}, use_global_device_ids=true, to_apply=%region_9.10 | all-reduce | flops 4352 | bytes 34816 | tf_op jit(solution)/shard_map/psum | solution.py:149
  (139 shorter events, 79.4 us)
Async XLA Ops:
  7.2 99.0 %all-gather.4.cloned.1.call-start = ((), (), s32[]{:S(2)}) async-start(), calls=%async_computation.4 | async-start | bytes 4456448 | tf_op jit(solution)/shard_map/all_gather | solution.py:94
  11.1 139.5 %all-gather.6.cloned.1.call-start = ((), (), s32[]{:S(2)}) async-start(), calls=%async_computation.7 | async-start | bytes 4456448 | tf_op jit(solution)/shard_map/all_gather | solution.py:121
  11.9 6.8 %copy-start.21 = (f32[3,3,256]{2,1,0:T(4,128)S(1)}, f32[3,3,256]{2,1,0:T(4,128)}, u32[]{:S(2)}) copy-start(f32[3,3,256]{2,1,0:T(4,128)} %param.9) | copy-start | bytes 27652
  11.9 452.4 %reduce-scatter.5.cloned.1.call-start = ((), (), s32[]{:S(2)}) async-start(), calls=%async_computation.6 | async-start | bytes 2228224 | tf_op jit(solution)/shard_map/reduce_scatter | solution.py:158
  16.7 85.3 %collective-permute-start = (bf16[2048,3,256]{0,2,1:T(8,128)(2,1)}, bf16[2048,3,256]{0,2,1:T(8,128)(2,1)}, u32[]{:S(2)}, u32[]{:S(2)}) collective-permute-start(bf16[2048,3,256]{0,2,1:T(8,128)(2,1)} %copy.21), channel_id=1, source_target_pairs={{0,128},{128,0},{1,129},{129,1},{2,130},{130,2},{3,131},{131,3},{4... | collective-permute-start | bytes 9437192 | tf_op jit(solution)/shard_map/ppermute | solution.py:20
  17.5 108.7 %collective-permute-start.3 = (bf16[256,2048]{1,0:T(8,128)(2,1)}, bf16[256,2048]{1,0:T(8,128)(2,1)}, u32[]{:S(2)}, u32[]{:S(2)}) collective-permute-start(bf16[256,2048]{1,0:T(8,128)(2,1)} %param.8), channel_id=1, source_target_pairs={{0,128},{128,0},{1,129},{129,1},{2,130},{130,2},{3,131},{131,3},{4... | collective-permute-start | bytes 3145736 | tf_op jit(solution)/shard_map/ppermute | solution.py:20
  113.7 15.3 %copy-start.6 = (bf16[512,768]{1,0:T(8,128)(2,1)}, bf16[512,768]{1,0:T(8,128)(2,1)S(1)}, u32[]{:S(2)}) copy-start(bf16[512,768]{1,0:T(8,128)(2,1)S(1)} %convolution_convert_fusion.3) | copy-start | bytes 2359300
  113.9 15.1 %collective-permute-start.1 = (bf16[2,3,256]{0,2,1:T(8,128)(2,1)S(1)}, bf16[2,3,256]{0,2,1:T(8,128)(2,1)}, u32[]{:S(2)}, u32[]{:S(2)}) collective-permute-start(bf16[2,3,256]{0,2,1:T(8,128)(2,1)S(1)} %bitcast.156), channel_id=1, source_target_pairs={{0,16},{16,32},{32,48},{48,64},{64,80},{80,96},{96,112},{1,17},{17... | collective-permute-start | bytes 9224 | tf_op jit(solution)/shard_map/ppermute | solution.py:12
  134.2 22.4 %copy-start.19 = (f32[128,16]{0,1:T(8,128)S(1)}, f32[128,16]{0,1:T(8,128)}, u32[]{:S(2)}) copy-start(f32[128,16]{0,1:T(8,128)} %param.10) | copy-start | bytes 24580
  155.1 10.9 %copy-start.8 = (bf16[512,256]{0,1:T(8,128)(2,1)}, bf16[512,256]{0,1:T(8,128)(2,1)S(1)}, u32[]{:S(2)}) copy-start(bf16[512,256]{0,1:T(8,128)(2,1)S(1)} %get-tuple-element.17) | copy-start | bytes 786436
  155.1 13.7 %collective-permute-start.4 = (bf16[127,256]{0,1:T(8,128)(2,1)S(1)}, bf16[127,256]{0,1:T(8,128)(2,1)S(1)}, u32[]{:S(2)}, u32[]{:S(2)}) collective-permute-start(bf16[127,256]{0,1:T(8,128)(2,1)S(1)} %slice.125), channel_id=1, source_target_pairs={{16,0},{32,16},{48,32},{64,48},{80,64},{96,80},{112,96},{17,1},{33... | collective-permute-start | bytes 195080 | tf_op jit(solution)/shard_map/ppermute | solution.py:12
  181.0 16.6 %collective-permute-start.2 = (bf16[127,256]{0,1:T(8,128)(2,1)}, bf16[127,256]{0,1:T(8,128)(2,1)}, u32[]{:S(2)}, u32[]{:S(2)}) collective-permute-start(bf16[127,256]{0,1:T(8,128)(2,1)} %slice_bitcast_fusion.1), channel_id=1, source_target_pairs={{0,16},{16,32},{32,48},{48,64},{64,80},{80,96},{96,112},{1,17},{17... | collective-permute-start | bytes 195080 | tf_op jit(solution)/shard_map/ppermute | solution.py:12
  207.6 4.6 copy-start.11
  207.6 7.3 %copy-start.4 = (bf16[1,512,4096]{2,1,0:T(8,128)(2,1)S(1)}, bf16[1,512,4096]{2,1,0:T(8,128)(2,1)}, u32[]{:S(2)}) copy-start(bf16[1,512,4096]{2,1,0:T(8,128)(2,1)} %all-gather.6.cloned.1.call-done) | copy-start | bytes 12582916
  217.5 246.8 %reduce-scatter.3.cloned.1.call-start = ((), (), s32[]{:S(2)}) async-start(), calls=%async_computation.5 | async-start | bytes 6684672 | tf_op jit(solution)/shard_map/reduce_scatter | solution.py:155
  217.6 15.8 %copy-start.1 = (f32[512,1,256]{0,2,1:T(8,128)S(1)}, f32[512,1,256]{0,2,1:T(8,128)}, u32[]{:S(2)}) copy-start(f32[512,1,256]{0,2,1:T(8,128)} %get-tuple-element.24) | copy-start | bytes 1572868
  218.9 14.6 %copy-start = (f32[512,768]{0,1:T(8,128)S(1)}, f32[512,768]{0,1:T(8,128)}, u32[]{:S(2)}) copy-start(f32[512,768]{0,1:T(8,128)} %copy.23) | copy-start | bytes 4718596
  218.9 14.4 %collective-permute-start.5 = (f32[2,3,256]{0,2,1:T(8,128)S(1)}, f32[2,3,256]{0,2,1:T(8,128)S(1)}, u32[]{:S(2)}, u32[]{:S(2)}) collective-permute-start(f32[2,3,256]{0,2,1:T(8,128)S(1)} %slice.128), channel_id=1, source_target_pairs={{16,0},{32,16},{48,32},{64,48},{80,64},{96,80},{112,96},{17,1},{33... | collective-permute-start | bytes 18440 | tf_op jit(solution)/shard_map/ppermute | solution.py:12
  233.5 4.3 copy-start.25
  247.5 6.9 %copy-start.18 = (bf16[512,3,256]{0,2,1:T(8,128)(2,1)S(1)}, bf16[512,3,256]{0,2,1:T(8,128)(2,1)}, u32[]{:S(2)}) copy-start(bf16[512,3,256]{0,2,1:T(8,128)(2,1)} %copy-done.17) | copy-start | bytes 2359300
  247.5 127.9 %all-to-all-start = ((bf16[16,32,4096]{2,1,0:T(8,128)(2,1)}), bf16[16,32,4096]{2,1,0:T(8,128)(2,1)}, u32[]{:S(2)}, u32[]{:S(2)}) async-start(bf16[16,32,4096]{2,1,0:T(8,128)(2,1)} %bitcast.143), calls=%async_computation | async-start | bytes 8388608 | tf_op jit(solution)/shard_map/all_to_all | solution.py:36
  375.3 8.2 %copy-start.9 = (bf16[512,256]{0,1:T(8,128)(2,1)S(1)}, bf16[512,256]{0,1:T(8,128)(2,1)}, u32[]{:S(2)}) copy-start(bf16[512,256]{0,1:T(8,128)(2,1)} %copy-done.8) | copy-start | bytes 786436
  375.3 8.2 %copy-start.3 = (f32[4,256,16,16]{1,3,0,2:T(8,128)S(1)}, f32[4,256,16,16]{1,3,0,2:T(8,128)}, u32[]{:S(2)}) copy-start(f32[4,256,16,16]{1,3,0,2:T(8,128)} %copy_dynamic-update-slice_fusion) | copy-start | bytes 3145732
  375.3 84.7 %all-to-all-start.1 = ((bf16[16,32,4096]{2,1,0:T(8,128)(2,1)}), bf16[16,32,4096]{2,1,0:T(8,128)(2,1)}, u32[]{:S(2)}, u32[]{:S(2)}) async-start(bf16[16,32,4096]{2,1,0:T(8,128)(2,1)} %bitcast.153), calls=%async_computation.1 | async-start | bytes 8388608 | tf_op jit(solution)/shard_map/all_to_all | solution.py:36
  (16 other events, 31.1 us)
Sparse Core Ops, SparseCore 0:
  11.3 75.7 all-gather.3
  89.8 60.7 all-gather.5
  217.6 73.3 reduce-scatter.4
  294.0 83.9 reduce-scatter.2
where the time goes:
time: 472 us; the launch traced here: 471 us
  waiting for transfers between devices  225 us (48%)
  local copies, waits for them, and re-layouts  71.6 us (15%)
  blocking collectives  62.8 us (13%)
  matrix products  40.4 us (9%)
  starting transfers between devices  30.1 us (6%)
  other arithmetic  26.6 us (6%)
  between operations  14.2 us (3%)
    all_to_all x2, waiting for transfers between devices, scatter_sum(): pieces = lax.all_to_all(value.reshape(split), axis, dim, 0)  113 us
    ppermute x2, waiting for transfers between devices, pair_gather(): lax.ppermute(value, axis, [(i, (i + step) % count) for i in range(count)])  82.2 us
    psum x1, blocking collectives, per_device(): lax.psum((short_term, mixer_term), ('dp', 'context'))  62.8 us
    all_gather x1, waiting for transfers between devices, per_device(): cot_slab = lax.all_gather(cotangent[0], 'tensor', axis=0, tiled=True)  16.4 us
    unnamed x60, local copies, waits for them, and re-layouts  16.3 us
    all_to_all x2, starting transfers between devices, scatter_sum(): pieces = lax.all_to_all(value.reshape(split), axis, dim, 0)  15.1 us
    ppermute x4, starting transfers between devices, from_behind(): lax.ppermute(value, axis, [(source, source + steps) for source in range(i...  12.9 us
    ppermute x4, waiting for transfers between devices, from_behind(): lax.ppermute(value, axis, [(source, source + steps) for source in range(i...  12.7 us
  transfers between devices with their start and end apart: 12, of which 5 were waited for; matrix products, arithmetic and copies ran while one was open for 20% of the time, Pallas kernels for 0%

commit v1 on v0

--- a/solution.py
+++ b/solution.py
@@ -118,7 +118,11 @@
         0,
     )
     block_out = (own + branch).astype(jnp.bfloat16)[None]
-    cot_slab = lax.all_gather(cotangent[0], "tensor", axis=0, tiled=True)
+    payload = cotangent[0]
+    cards = []
+    for _ in range(lax.psum(1, "tensor")):
+        cards.append(payload)
+    cot_slab = jnp.concatenate(lax.all_to_all(jnp.stack(cards, 0), "tensor", 0, 0), 0)
     grad_rows = lax.dot_general(
         cot_slab, full_out, (((1,), (1,)), ((), ())), preferred_element_type=jnp.float32
     )

time: 472 us -> 496 us (1.051)
  waiting for transfers between devices: 225 us -> 238 us
  starting transfers between devices: 30.1 us -> 36.9 us
    ppermute x2, waiting for transfers between devices: 82.2 us -> 115 us  [pair_gather(): lax.ppermute(value, axis, [(i, (i + step) % count) for i in range(count)])]
    all_gather x1 -> x0, waiting for transfers between devices: 16.4 us -> none  [per_device(): cot_slab = lax.all_gather(cotangent[0], 'tensor', axis=0, tiled=True)]
    all_to_all x0 -> x1, starting transfers between devices: none -> 7.58 us  [per_device(): lax.all_to_all(jnp.stack(cards, 0), 'tensor', 0, 0)]
    unnamed x60 -> x52, local copies, waits for them, and re-layouts: 16.3 us -> 13.9 us
  transfers between devices with their start and end apart: 12 -> 12, of which waited for: 5 -> 4; matrix products, arithmetic and copies ran while one was open for 20% -> 19% of each run, Pallas kernels for 0% -> 0%
where the time goes in v1:
time: 496 us; the launch traced here: 494 us
  waiting for transfers between devices  238 us (48%)
  local copies, waits for them, and re-layouts  69.1 us (14%)
  blocking collectives  66.6 us (13%)
  matrix products  43.9 us (9%)
  starting transfers between devices  36.9 us (7%)
  other arithmetic  25.6 us (5%)
  between operations  14.2 us (3%)
    ppermute x2, waiting for transfers between devices, pair_gather(): lax.ppermute(value, axis, [(i, (i + step) % count) for i in range(count)])  115 us
    all_to_all x2, waiting for transfers between devices, scatter_sum(): pieces = lax.all_to_all(value.reshape(split), axis, dim, 0)  113 us
    psum x1, blocking collectives, per_device(): lax.psum((short_term, mixer_term), ('dp', 'context'))  66.6 us
    all_to_all x2, starting transfers between devices, scatter_sum(): pieces = lax.all_to_all(value.reshape(split), axis, dim, 0)  14.8 us
    unnamed x52, local copies, waits for them, and re-layouts  13.9 us
    ppermute x4, starting transfers between devices, from_behind(): lax.ppermute(value, axis, [(source, source + steps) for source in range(i...  12.3 us
    another operation x4, local copies, waits for them, and re-layouts, skew_table(): jnp.tile(padded[:, None, :], (1, span, 1))  11.6 us
    dynamic_update_slice x4, local copies, waits for them, and re-layouts, pair_gather(): full = lax.dynamic_update_slice(full, part, start)  10.7 us
  transfers between devices with their start and end apart: 12, of which 4 were waited for; matrix products, arithmetic and copies ran while one was open for 19% of the time, Pallas kernels for 0%

profile of v1, /device:TPU:6, one launch (start us, length us, event | category | flops | bytes accessed | tf_op | source)
XLA Modules:
  0.0 493.9 jit_solution(9462856654877208316)
XLA Ops:
  11.2 4.7 copy.21
  19.3 7.6 %all-to-all-start.1 = ((bf16[16,32,4096]{2,1,0:T(8,128)(2,1)}), bf16[16,32,4096]{2,1,0:T(8,128)(2,1)}, u32[]{:S(2)}, u32[]{:S(2)}) async-start(bf16[16,32,4096]{2,1,0:T(8,128)(2,1)} %stack.25), calls=%async_computation.1 | async-start | bytes 8388608 | tf_op jit(solution)/shard_map/all_to_all | solution.py:125
  33.3 4.0 constant_dynamic-update-slice_fusion.3
  37.4 63.9 %collective-permute-done = bf16[2048,3,256]{0,2,1:T(8,128)(2,1)} collective-permute-done((bf16[2048,3,256]{0,2,1:T(8,128)(2,1)}, bf16[2048,3,256]{0,2,1:T(8,128)(2,1)}, u32[]{:S(2)}, u32[]{:S(2)}) %collective-permute-start) | collective-permute-done | bytes 3145760 | tf_op jit(solution)/shard_map/ppermute | solution.py:20
  101.3 4.1 constant_dynamic-update-slice_fusion.2
  105.4 7.5 %convolution_convert_fusion.3 = bf16[512,768]{1,0:T(8,128)(2,1)S(1)} fusion(bf16[512,4096]{1,0:T(8,128)(2,1)} %all-gather.2.cloned.1.call-done, bf16[4096,768]{0,1:T(8,128)(2,1)} %bitcast.1), kind=kOutput, calls=%fused_computation.26 | convolution fusion | flops 3221618688 | bytes 11272192 | tf_op jit(solution)/shard_map/dot_general | solution.py:99
  113.1 4.5 collective-permute-start.1
  117.6 50.9 %collective-permute-done.3 = bf16[256,2048]{1,0:T(8,128)(2,1)} collective-permute-done((bf16[256,2048]{1,0:T(8,128)(2,1)}, bf16[256,2048]{1,0:T(8,128)(2,1)}, u32[]{:S(2)}, u32[]{:S(2)}) %collective-permute-start.3) | collective-permute-done | bytes 1048608 | tf_op jit(solution)/shard_map/ppermute | solution.py:20
  172.2 4.2 multiply_add_fusion
  176.5 4.4 fusion.40
  184.4 3.9 tile.17
  198.7 3.9 fusion.12
  206.2 4.5 collective-permute-start.2
  212.8 3.9 tile.15
  228.1 4.2 fusion.9
  233.5 5.1 %convolution_convert_fusion.2 = bf16[256,4096]{1,0:T(8,128)(2,1)} fusion(bf16[512,4096]{1,0:T(8,128)(2,1)} %bitcast.13, f32[512,1,256]{0,2,1:T(8,128)} %reshape.155, f32[512,3,256]{0,2,1:T(8,128)} %multiply_add_fusion), kind=kOutput, calls=%fused_computation.5 | convolution fusion | flops 1075052544 | bytes 7340032 | tf_op jit(solution)/shard_map/dot_general | solution.py:129
  243.0 10.2 %collective-permute-done.5 = f32[2,3,256]{0,2,1:T(8,128)S(1)} collective-permute-done((f32[2,3,256]{0,2,1:T(8,128)S(1)}, f32[2,3,256]{0,2,1:T(8,128)S(1)}, u32[]{:S(2)}, u32[]{:S(2)}) %collective-permute-start.5) | collective-permute-done | bytes 6176 | tf_op jit(solution)/shard_map/ppermute | solution.py:12
  257.7 5.4 %convolution_convert_fusion = bf16[4096,3,256]{2,0,1:T(8,128)(2,1)} fusion(bf16[512,4096]{1,0:T(8,128)(2,1)S(1)} %copy-done.21, bf16[512,3,256]{0,2,1:T(8,128)(2,1)S(1)} %get-tuple-element.20), kind=kOutput, calls=%fused_computation.3 | convolution fusion | flops 3224371200 | bytes 11272192 | tf_op jit(solution)/shard_map/dot_general | solution.py:155
  263.1 4.4 convolution_convert_fusion.1
  267.5 7.3 %all-to-all-start = ((bf16[16,32,4096]{2,1,0:T(8,128)(2,1)}), bf16[16,32,4096]{2,1,0:T(8,128)(2,1)}, u32[]{:S(2)}, u32[]{:S(2)}) async-start(bf16[16,32,4096]{2,1,0:T(8,128)(2,1)} %bitcast.142), calls=%async_computation | async-start | bytes 8388608 | tf_op jit(solution)/shard_map/all_to_all | solution.py:36
  274.8 7.9 %bitcast_convert_fusion = bf16[512,4096]{1,0:T(8,128)(2,1)} fusion(bf16[512,3,256]{0,2,1:T(8,128)(2,1)S(1)} %copy-done.13, bf16[4096,3,256]{0,2,1:T(8,128)(2,1)} %constant_dynamic-update-slice_fusion.2), kind=kOutput, calls=%fused_computation | convolution fusion | flops 3223322624 | bytes 11272192 | tf_op jit(solution)/shard_map/dot_general | solution.py:168
  282.7 112.5 %all-to-all-done = bf16[16,32,4096]{2,1,0:T(8,128)(2,1)} async-done(((bf16[16,32,4096]{2,1,0:T(8,128)(2,1)}), bf16[16,32,4096]{2,1,0:T(8,128)(2,1)}, u32[]{:S(2)}, u32[]{:S(2)}) %all-to-all-start) | async-done | bytes 4194336 | tf_op jit(solution)/shard_map/all_to_all | solution.py:36
  395.2 7.5 %all-to-all-start.2 = ((bf16[16,32,4096]{2,1,0:T(8,128)(2,1)}), bf16[16,32,4096]{2,1,0:T(8,128)(2,1)}, u32[]{:S(2)}, u32[]{:S(2)}) async-start(bf16[16,32,4096]{2,1,0:T(8,128)(2,1)} %bitcast.154), calls=%async_computation.2 | async-start | bytes 8388608 | tf_op jit(solution)/shard_map/all_to_all | solution.py:36
  412.8 66.6 %all-reduce.4 = (f32[3,3,256]{2,0,1:T(4,128)S(1)}, f32[128,16]{0,1:T(8,128)}) all-reduce(f32[3,3,256]{2,0,1:T(4,128)S(1)} %pad_maximum_fusion.4, f32[128,16]{0,1:T(8,128)S(1)} %bitcast.160), channel_id=1, replica_groups=mesh['dp'=2,'context'=8,'tensor'=16] {'dp','context'}, use_global_device_ids=true, to_apply=%region_9.10 | all-reduce | flops 4352 | bytes 34816 | tf_op jit(solution)/shard_map/psum | solution.py:153
  (132 shorter events, 76.4 us)
Async XLA Ops:
  7.2 98.2 %all-gather.2.cloned.1.call-start = ((), (), s32[]{:S(2)}) async-start(), calls=%async_computation.5 | async-start | bytes 4456448 | tf_op jit(solution)/shard_map/all_gather | solution.py:94
  11.2 5.6 %copy-start.10 = (bf16[1,32,4096]{2,1,0:T(8,128)(2,1)S(1)}, bf16[1,32,4096]{2,1,0:T(8,128)(2,1)}, u32[]{:S(2)}) copy-start(bf16[1,32,4096]{2,1,0:T(8,128)(2,1)} %param.11) | copy-start | bytes 786436
  16.0 85.3 %collective-permute-start = (bf16[2048,3,256]{0,2,1:T(8,128)(2,1)}, bf16[2048,3,256]{0,2,1:T(8,128)(2,1)}, u32[]{:S(2)}, u32[]{:S(2)}) collective-permute-start(bf16[2048,3,256]{0,2,1:T(8,128)(2,1)} %copy.21), channel_id=1, source_target_pairs={{0,128},{128,0},{1,129},{129,1},{2,130},{130,2},{3,131},{131,3},{4... | collective-permute-start | bytes 9437192 | tf_op jit(solution)/shard_map/ppermute | solution.py:20
  19.3 8.9 %copy-start.17 = (f32[3,3,256]{2,1,0:T(4,128)S(1)}, f32[3,3,256]{2,1,0:T(4,128)}, u32[]{:S(2)}) copy-start(f32[3,3,256]{2,1,0:T(4,128)} %param.9) | copy-start | bytes 27652
  19.3 157.1 %all-to-all-start.1 = ((bf16[16,32,4096]{2,1,0:T(8,128)(2,1)}), bf16[16,32,4096]{2,1,0:T(8,128)(2,1)}, u32[]{:S(2)}, u32[]{:S(2)}) async-start(bf16[16,32,4096]{2,1,0:T(8,128)(2,1)} %stack.25), calls=%async_computation.1 | async-start | bytes 8388608 | tf_op jit(solution)/shard_map/all_to_all | solution.py:125
  26.9 460.4 %reduce-scatter.5.cloned.1.call-start = ((), (), s32[]{:S(2)}) async-start(), calls=%async_computation.7 | async-start | bytes 2228224 | tf_op jit(solution)/shard_map/reduce_scatter | solution.py:162
  27.0 141.5 %collective-permute-start.3 = (bf16[256,2048]{1,0:T(8,128)(2,1)}, bf16[256,2048]{1,0:T(8,128)(2,1)}, u32[]{:S(2)}, u32[]{:S(2)}) collective-permute-start(bf16[256,2048]{1,0:T(8,128)(2,1)} %param.8), channel_id=1, source_target_pairs={{0,128},{128,0},{1,129},{129,1},{2,130},{130,2},{3,131},{131,3},{4... | collective-permute-start | bytes 3145736 | tf_op jit(solution)/shard_map/ppermute | solution.py:20
  112.9 58.4 %copy-start.5 = (bf16[512,768]{1,0:T(8,128)(2,1)}, bf16[512,768]{1,0:T(8,128)(2,1)S(1)}, u32[]{:S(2)}) copy-start(bf16[512,768]{1,0:T(8,128)(2,1)S(1)} %convolution_convert_fusion.3) | copy-start | bytes 2359300
  113.1 58.2 %collective-permute-start.1 = (bf16[2,3,256]{0,2,1:T(8,128)(2,1)S(1)}, bf16[2,3,256]{0,2,1:T(8,128)(2,1)}, u32[]{:S(2)}, u32[]{:S(2)}) collective-permute-start(bf16[2,3,256]{0,2,1:T(8,128)(2,1)S(1)} %bitcast.157), channel_id=1, source_target_pairs={{0,16},{16,32},{32,48},{48,64},{64,80},{80,96},{96,112},{1,17},{17... | collective-permute-start | bytes 9224 | tf_op jit(solution)/shard_map/ppermute | solution.py:12
  176.5 6.0 %copy-start.14 = (f32[128,16]{0,1:T(8,128)S(1)}, f32[128,16]{0,1:T(8,128)}, u32[]{:S(2)}) copy-start(f32[128,16]{0,1:T(8,128)} %param.10) | copy-start | bytes 24580
  180.9 10.9 %copy-start.7 = (bf16[512,256]{0,1:T(8,128)(2,1)}, bf16[512,256]{0,1:T(8,128)(2,1)S(1)}, u32[]{:S(2)}) copy-start(bf16[512,256]{0,1:T(8,128)(2,1)S(1)} %get-tuple-element.17) | copy-start | bytes 786436
  180.9 13.8 %collective-permute-start.4 = (bf16[127,256]{0,1:T(8,128)(2,1)S(1)}, bf16[127,256]{0,1:T(8,128)(2,1)S(1)}, u32[]{:S(2)}, u32[]{:S(2)}) collective-permute-start(bf16[127,256]{0,1:T(8,128)(2,1)S(1)} %slice.125), channel_id=1, source_target_pairs={{16,0},{32,16},{48,32},{64,48},{80,64},{96,80},{112,96},{17,1},{33... | collective-permute-start | bytes 195080 | tf_op jit(solution)/shard_map/ppermute | solution.py:12
  203.8 7.0 %copy-start.15 = (f32[128,16]{0,1:T(8,128)S(1)}, f32[128,16]{0,1:T(8,128)}, u32[]{:S(2)}) copy-start(f32[128,16]{0,1:T(8,128)} %param.10) | copy-start | bytes 24580
  206.2 14.0 %collective-permute-start.2 = (bf16[127,256]{0,1:T(8,128)(2,1)S(1)}, bf16[127,256]{0,1:T(8,128)(2,1)S(1)}, u32[]{:S(2)}, u32[]{:S(2)}) collective-permute-start(bf16[127,256]{0,1:T(8,128)(2,1)S(1)} %slice_bitcast_fusion), channel_id=1, source_target_pairs={{0,16},{16,32},{32,48},{48,64},{64,80},{80,96},{96,112},{1,17},{17... | collective-permute-start | bytes 195080 | tf_op jit(solution)/shard_map/ppermute | solution.py:12
  238.7 248.7 %reduce-scatter.3.cloned.1.call-start = ((), (), s32[]{:S(2)}) async-start(), calls=%async_computation.6 | async-start | bytes 6684672 | tf_op jit(solution)/shard_map/reduce_scatter | solution.py:159
  239.8 13.3 %copy-start.1 = (f32[512,1,256]{0,2,1:T(8,128)S(1)}, f32[512,1,256]{0,2,1:T(8,128)}, u32[]{:S(2)}) copy-start(f32[512,1,256]{0,2,1:T(8,128)} %get-tuple-element.19) | copy-start | bytes 1572868
  241.2 12.1 %copy-start = (f32[512,768]{0,1:T(8,128)S(1)}, f32[512,768]{0,1:T(8,128)}, u32[]{:S(2)}) copy-start(f32[512,768]{0,1:T(8,128)} %copy.23) | copy-start | bytes 4718596
  241.2 12.0 %collective-permute-start.5 = (f32[2,3,256]{0,2,1:T(8,128)S(1)}, f32[2,3,256]{0,2,1:T(8,128)S(1)}, u32[]{:S(2)}, u32[]{:S(2)}) collective-permute-start(f32[2,3,256]{0,2,1:T(8,128)S(1)} %slice.128), channel_id=1, source_target_pairs={{16,0},{32,16},{48,32},{64,48},{80,64},{96,80},{112,96},{17,1},{33... | collective-permute-start | bytes 18440 | tf_op jit(solution)/shard_map/ppermute | solution.py:12
  253.3 4.3 copy-start.21
  267.5 7.3 %copy-start.13 = (bf16[512,3,256]{0,2,1:T(8,128)(2,1)S(1)}, bf16[512,3,256]{0,2,1:T(8,128)(2,1)}, u32[]{:S(2)}) copy-start(bf16[512,3,256]{0,2,1:T(8,128)(2,1)} %copy-done.12) | copy-start | bytes 2359300
  267.5 127.7 %all-to-all-start = ((bf16[16,32,4096]{2,1,0:T(8,128)(2,1)}), bf16[16,32,4096]{2,1,0:T(8,128)(2,1)}, u32[]{:S(2)}, u32[]{:S(2)}) async-start(bf16[16,32,4096]{2,1,0:T(8,128)(2,1)} %bitcast.142), calls=%async_computation | async-start | bytes 8388608 | tf_op jit(solution)/shard_map/all_to_all | solution.py:36
  395.2 7.5 %copy-start.8 = (bf16[512,256]{0,1:T(8,128)(2,1)S(1)}, bf16[512,256]{0,1:T(8,128)(2,1)}, u32[]{:S(2)}) copy-start(bf16[512,256]{0,1:T(8,128)(2,1)} %copy-done.7) | copy-start | bytes 786436
  395.2 7.6 %copy-start.3 = (f32[4,256,16,16]{1,3,0,2:T(8,128)S(1)}, f32[4,256,16,16]{1,3,0,2:T(8,128)}, u32[]{:S(2)}) copy-start(f32[4,256,16,16]{1,3,0,2:T(8,128)} %copy_dynamic-update-slice_fusion) | copy-start | bytes 3145732
  395.2 87.8 %all-to-all-start.2 = ((bf16[16,32,4096]{2,1,0:T(8,128)(2,1)}), bf16[16,32,4096]{2,1,0:T(8,128)(2,1)}, u32[]{:S(2)}, u32[]{:S(2)}) async-start(bf16[16,32,4096]{2,1,0:T(8,128)(2,1)} %bitcast.154), calls=%async_computation.2 | async-start | bytes 8388608 | tf_op jit(solution)/shard_map/all_to_all | solution.py:36
  (12 other events, 26.8 us)
Sparse Core Ops, SparseCore 0:
  11.3 82.6 all-gather.1
  238.8 77.2 reduce-scatter.4
  319.2 84.1 reduce-scatter.2
